TPU v7x, 256 devices: a whole 4x4x8 slice. The times are simulated.
256 devices in a mesh: region: 64 (over x, z, core), level: 4 (over y).
Axes of the slice: x: 4, y: 4, z: 8, core: 2. Of those that a mesh axis runs over, the one named last changes fastest.
Arguments:
- ensemble: bfloat16 [4, 256, 262144], P('level', None, 'region'), may hold values from -6 to 6
- obs_anomaly: bfloat16 [4, 65536, 256], P('level', 'region'), may hold values from -6 to 6
- innovation: bfloat16 [4, 65536], P('level', 'region'), may hold values from -18 to 18
- obs_precision: bfloat16 [4, 65536], P('level', 'region'), may hold values from 0.019897461 to 0.29882812
- owner_region: int32 [4, 65536, 1], P('level', 'region'), may hold values from 0 to 63; in each aligned block of 1024 rows (0 to 1023, 1024 to 2047, ..., all dimensions but the last counted through in order) at most 24 rows name the same one
- neighbours: int32 [64, 3], replicated, may hold values from 0 to 63, all different within a row
Outputs:
- analysis: bfloat16 [4, 256, 262144], P('level', None, 'region')
Inputs may be any that keep to these rules, and one draw needn't show every extreme that they name: `owner_region`: among the 1024 observations of one device (aligned blocks), no region is named more than 24 times, a bound that some block reaches. `neighbours`: each row lists 3 different regions; every region is listed by some row.
All inputs are finite; a program needn't handle non-finite values.
Results may differ from a plain program's by a relative error of at most 0.0059.
Values may be sent and summed in bfloat16 or wider, within the bound.
No kernel may reach another device: no remote copies, remote signals or barrier semaphores. Data moves between devices by JAX's collectives and lax.ppermute only.
A program may use at most 64 MiB of HBM per device.

v0:
```python
import math
import jax
import jax.numpy as jnp
from jax import lax
from jax.sharding import PartitionSpec as P

NSTEPS = 4
TAPER = 0.6


def cut_along(value, dim, count):
    before, after = (value.shape[:dim], value.shape[dim + 1 :])
    return jnp.moveaxis(value.reshape(*before, count, -1, *after), dim, 0)


def sum_at_owner(value, axis, dim):
    count = lax.axis_size(axis)
    pieces = lax.all_to_all(cut_along(value, dim, count), axis, 0, 0, tiled=True)
    return jnp.sum(pieces, axis=0)


def neighbour_weights(neighbours):
    region_ids = jnp.arange(neighbours.shape[0], dtype=jnp.int32)
    weights = (region_ids[:, None] == region_ids[None, :]).astype(jnp.float32)
    for listed in range(neighbours.shape[1]):
        hit = (neighbours[:, listed][:, None] == region_ids[None, :]).astype(jnp.float32)
        weights = weights + TAPER ** (listed + 1) * hit
    return weights


def inverse_root(matrix):
    order_size = matrix.shape[0]
    identity = jnp.eye(order_size, dtype=jnp.float32)
    norm_scale = 0.5 * jnp.sqrt(jnp.sum(matrix * matrix))
    root_iter = matrix / norm_scale
    inverse_iter = identity
    for newton_step in range(NSTEPS):
        correction = 1.5 * identity - 0.5 * jnp.dot(
            inverse_iter, root_iter, precision=lax.Precision.HIGHEST
        )
        root_iter = jnp.dot(root_iter, correction, precision=lax.Precision.HIGHEST)
        inverse_iter = jnp.dot(correction, inverse_iter, precision=lax.Precision.HIGHEST)
    return inverse_iter / jnp.sqrt(norm_scale)


def analysis_weights(covariance, innovation_sum):
    order_size = covariance.shape[0]
    identity = jnp.eye(order_size, dtype=jnp.float32)
    precision_matrix = covariance + (order_size - 1.0) * identity
    root = inverse_root(precision_matrix)
    inner = jnp.dot(root, innovation_sum, precision=lax.Precision.HIGHEST)
    mean_shift = jnp.dot(root, inner, precision=lax.Precision.HIGHEST)
    return (math.sqrt(order_size - 1.0) * root + mean_shift[:, None]).astype(jnp.bfloat16)


def update_columns(column_block, transform):
    average = jnp.mean(column_block.astype(jnp.float32), axis=0)
    anomaly = (column_block.astype(jnp.float32) - average[None, :]).astype(jnp.bfloat16)
    combined = lax.dot_general(
        transform, anomaly, (((0,), (0,)), ((), ())), preferred_element_type=jnp.float32
    )
    return (combined + average[None, :]).astype(jnp.bfloat16)


def level_factor(distance, levels):
    factor = jnp.zeros(distance.shape, jnp.float32)
    for apart in range(levels):
        factor = factor + 0.5**apart * (distance == apart).astype(jnp.float32)
    return factor


def body(ensemble, obs_anomaly, innovation, obs_precision, owner_region, neighbours):
    regions = lax.axis_size("region")
    levels = lax.axis_size("level")
    my_level = lax.axis_index("level")
    members = obs_anomaly.shape[2]
    local_obs = obs_anomaly.shape[1]
    capacity = 3 * local_obs // (2 * regions)
    slot_count = (neighbours.shape[1] + 1) * capacity
    region_weight = neighbour_weights(neighbours)
    owner_ids = owner_region[0, :, 0]
    region_ids = jnp.arange(regions, dtype=jnp.int32)
    owner_table = (owner_ids[:, None] == region_ids[None, :]).astype(jnp.float32)
    dest_weight = jnp.dot(owner_table, region_weight.T, precision=lax.Precision.HIGHEST)
    live = dest_weight > 0
    position = jnp.cumsum(live.astype(jnp.int32), axis=0) - 1
    gain = (dest_weight * obs_precision[0].astype(jnp.float32)[:, None]).astype(jnp.bfloat16)
    slot_ids = jnp.arange(slot_count, dtype=jnp.int32)
    placement = jnp.logical_and(
        live.T[:, None, :], position.T[:, None, :] == slot_ids[None, :, None]
    )
    place_float = placement.astype(jnp.float32)
    send_rows = jnp.einsum(
        "rso,om->rsm",
        placement.astype(jnp.bfloat16),
        obs_anomaly[0],
        preferred_element_type=jnp.float32,
    ).astype(jnp.bfloat16)
    send_gain = jnp.einsum(
        "rso,or->rs", place_float, gain.astype(jnp.float32), precision=lax.Precision.HIGHEST
    ).astype(jnp.bfloat16)
    send_innov = jnp.einsum(
        "rso,o->rs", place_float, innovation[0].astype(jnp.float32), precision=lax.Precision.HIGHEST
    ).astype(jnp.bfloat16)
    received = (
        lax.all_to_all(send_rows, "region", split_axis=0, concat_axis=0, tiled=True),
        lax.all_to_all(send_gain, "region", split_axis=0, concat_axis=0, tiled=True),
        lax.all_to_all(send_innov, "region", split_axis=0, concat_axis=0, tiled=True),
    )
    routed_rows = received[0].reshape(-1, members)
    routed_gain = received[1].reshape(-1)
    routed_innov = received[2].reshape(-1)
    weighted = (routed_gain.astype(jnp.float32)[:, None] * routed_rows.astype(jnp.float32)).astype(
        jnp.bfloat16
    )
    own_cov = jnp.dot(weighted.T, routed_rows, preferred_element_type=jnp.float32)
    own_sum = jnp.dot(routed_innov, weighted, preferred_element_type=jnp.float32)
    stacked = jnp.tile(own_cov, (levels, 1))
    target_level = jnp.arange(members * lax.axis_size("level"), dtype=jnp.int32) // members
    factor = level_factor(jnp.abs(target_level - my_level), levels)
    covariance = sum_at_owner(factor[:, None] * stacked, "level", 0)
    level_ids = jnp.arange(levels, dtype=jnp.int32)
    sum_terms = level_factor(jnp.abs(level_ids - my_level), levels)[:, None] * own_sum[None, :]
    all_sums = lax.psum(sum_terms, "level")
    innovation_sum = lax.dynamic_index_in_dim(all_sums, my_level, 0, keepdims=False)
    transform = analysis_weights(covariance, innovation_sum)
    return update_columns(ensemble[0], transform)[None]


def solution(mesh):
    return jax.shard_map(
        body,
        mesh=mesh,
        in_specs=(
            P("level", None, "region"),
            P("level", "region", None),
            P("level", "region"),
            P("level", "region"),
            P("level", "region", None),
            P(),
        ),
        out_specs=P("level", None, "region"),
        check_vma=False,
    )
```

profile of v0, /device:TPU:2, one launch (start us, length us, event | category | flops | bytes accessed | tf_op | source)
XLA Modules:
  0.0 175.8 jit_solution(10290218327440279134)
XLA Ops:
  0.0 0.8 slice_bitcast_fusion.2
  0.8 0.7 convert_element_type.111
  1.5 1.2 fusion.32
  2.9 18.0 %reduce-window.6 = s32[64,8,128]{2,1,0:T(8,128)S(1)} reduce-window(s32[64,8,128]{2,1,0:T(8,128)S(1)} %bitcast.82, s32[]{:T(128)} %constant.70.clone.1), window={size=1x1x128 pad=0_0x0_0x127_0}, to_apply=%region_0.0 | reduce-window | flops 8323072 | bytes 524292 | tf_op jit(solution)/shard_map/reduce-window
  21.5 4.8 %fusion.5 = f32[64,1,96]{2,1,0:T(1,128)S(1)} fusion(s32[64,1024]{1,0:T(8,128)S(1)} %bitcast.84, pred[64,1024]{1,0:T(8,128)(4,1)S(1)} %get-tuple-element.6, bf16[1024,64,1]{0,1,2:T(8,128)(2,1)S(1)} %fusion.37), kind=kOutput, calls=%fused_computation.4 | convolution fusion | flops 25165824 | bytes 483328 | tf_op jit(solution)/shard_map/rso,or->rs/dot_general | solution.py:99
  26.2 0.6 copy.17
  26.9 12.0 %all-to-all-start = ((bf16[64,1,96]{2,1,0:T(2,128)(2,1)}), bf16[64,1,96]{2,1,0:T(2,128)(2,1)S(1)}, u32[]{:S(2)}, u32[]{:S(2)}) async-start(bf16[64,1,96]{2,1,0:T(2,128)(2,1)} %copy.17), calls=%async_computation | async-start | bytes 65536 | tf_op jit(solution)/shard_map/all_to_all | solution.py:107
  38.9 6.9 %fusion.21 = bf16[64,96,256]{2,1,0:T(8,128)(2,1)} fusion(s32[64,1024]{1,0:T(8,128)S(1)} %bitcast.85, pred[64,1024]{1,0:T(8,128)(4,1)S(1)} %get-tuple-element.6, bf16[1,1024,256]{2,1,0:T(8,128)(2,1)S(1)} %copy-done), kind=kOutput, calls=%fused_computation.23 | convolution fusion | flops 3235381248 | bytes 3997696 | tf_op jit(solution)/shard_map/rso,om->rsm/dot_general | solution.py:93
  45.8 1.7 all-to-all-done
  47.5 9.0 %all-to-all-start.1 = ((bf16[64,96,256]{2,1,0:T(8,128)(2,1)}), bf16[64,96,256]{2,1,0:T(8,128)(2,1)}, u32[]{:S(2)}, u32[]{:S(2)}) async-start(bf16[64,96,256]{2,1,0:T(8,128)(2,1)} %fusion.21), calls=%async_computation.1 | async-start | bytes 6291456 | tf_op jit(solution)/shard_map/all_to_all | solution.py:106
  56.5 4.7 %fusion.1 = f32[1,64,96]{2,0,1:T(1,128)S(1)} fusion(s32[64,1024]{1,0:T(8,128)S(1)} %bitcast.86, pred[64,1024]{1,0:T(8,128)(4,1)S(1)} %get-tuple-element.6, bf16[1,1024]{1,0:T(2,128)(2,1)S(1)} %copy-done.2), kind=kOutput, calls=%fused_computation.2 | convolution fusion | flops 25165824 | bytes 354304 | tf_op jit(solution)/shard_map/rso,o->rs/dot_general | solution.py:102
  61.2 0.6 copy.18
  62.2 66.1 %all-to-all-done.1 = bf16[64,96,256]{2,1,0:T(8,128)(2,1)} async-done(((bf16[64,96,256]{2,1,0:T(8,128)(2,1)}), bf16[64,96,256]{2,1,0:T(8,128)(2,1)}, u32[]{:S(2)}, u32[]{:S(2)}) %all-to-all-start.1) | async-done | bytes 3145760 | tf_op jit(solution)/shard_map/all_to_all | solution.py:106
  128.3 7.3 %all-to-all-start.3 = ((bf16[64,1,96]{2,1,0:T(2,128)(2,1)}), bf16[64,1,96]{2,1,0:T(2,128)(2,1)S(1)}, u32[]{:S(2)}, u32[]{:S(2)}) async-start(bf16[64,1,96]{2,1,0:T(2,128)(2,1)} %copy.18), calls=%async_computation.3 | async-start | bytes 65536 | tf_op jit(solution)/shard_map/all_to_all | solution.py:108
  135.6 4.8 %fusion.30 = f32[256,256]{1,0:T(8,128)S(1)} fusion(bf16[64,96,256]{2,1,0:T(8,128)(2,1)} %all-to-all-done.1, f32[64,96]{1,0:T(8,128)S(1)} %bitcast.89), kind=kOutput, calls=%fused_computation.34 | convolution fusion | flops 810024960 | bytes 3432448 | tf_op jit(solution)/shard_map/dot_general | solution.py:116
  140.4 1.2 broadcast_multiply_fusion
  141.6 2.7 %all-to-all-done.3 = bf16[64,1,96]{2,1,0:T(2,128)(2,1)S(1)} async-done(((bf16[64,1,96]{2,1,0:T(2,128)(2,1)}), bf16[64,1,96]{2,1,0:T(2,128)(2,1)S(1)}, u32[]{:S(2)}, u32[]{:S(2)}) %all-to-all-start.3) | async-done | bytes 12320 | tf_op jit(solution)/shard_map/all_to_all | solution.py:108
  144.2 4.5 %all-to-all-start.2 = ((f32[4,256,256]{2,1,0:T(8,128)}), f32[4,256,256]{2,1,0:T(8,128)}, u32[]{:S(2)}, u32[]{:S(2)}) async-start(f32[4,256,256]{2,1,0:T(8,128)} %broadcast_multiply_fusion), calls=%async_computation.2 | async-start | bytes 2097152 | tf_op jit(solution)/shard_map/all_to_all | solution.py:18
  148.7 2.6 %fusion.15 = f32[1,256,1]{1,0,2:T(1,128)S(1)} fusion(bf16[64,96,256]{2,1,0:T(8,128)(2,1)} %all-to-all-done.1, f32[64,96]{1,0:T(8,128)S(1)} %bitcast.90, bf16[64,1,96]{2,1,0:T(2,128)(2,1)S(1)} %all-to-all-done.3), kind=kOutput, calls=%fused_computation.17 | convolution fusion | flops 7864320 | bytes 3183616 | tf_op jit(solution)/shard_map/dot_general | solution.py:117
  151.4 14.7 %psum.7 = f32[4,256]{1,0:T(4,128)S(1)} all-reduce(f32[4,256]{1,0:T(4,128)S(1)} %broadcast_multiply_fusion.2), channel_id=1, replica_groups=mesh['region'=64,'level'=4] {'level'}, use_global_device_ids=true, to_apply=%region_4.5 | all-reduce | flops 1024 | bytes 8192 | tf_op jit(solution)/shard_map/psum | solution.py:124
  166.1 1.3 reduce_sum.27
  167.4 0.7 multiply_reduce_fusion
  169.2 0.4 fusion.40
  169.9 0.4 fusion.28
  170.2 0.4 fusion.78
  170.6 0.4 fusion.77
  171.0 0.4 fusion.27
  171.4 0.4 fusion.79
  171.8 0.4 fusion.80
  172.2 0.4 fusion.26
  172.6 0.4 convolution_divide_fusion
  173.6 2.2 %fusion.14 = bf16[1,256,4096]{2,1,0:T(8,128)(2,1)} fusion(bf16[1,256,4096]{2,1,0:T(8,128)(2,1)S(1)} %copy-done.1, f32[4096]{0:T(1024)S(1)} %broadcast_multiply_fusion.1, f32[256,256]{1,0:T(8,128)S(1)} %convolution_divide_fusion, f32[256]{0:T(256)S(1)} %bitcast.93), kind=kOutput, calls=%fused_computation.16 | convolution fusion | flops 542310400 | bytes 4473856 | tf_op jit(solution)/shard_map/dot_general | solution.py:59
  (29 shorter events, 2.4 us)
Async XLA Ops:
  0.0 38.9 %copy-start = (bf16[1,1024,256]{2,1,0:T(8,128)(2,1)S(1)}, bf16[1,1024,256]{2,1,0:T(8,128)(2,1)}, u32[]{:S(2)}) copy-start(bf16[1,1024,256]{2,1,0:T(8,128)(2,1)} %param.7) | copy-start | bytes 1572868
  26.9 20.6 %all-to-all-start = ((bf16[64,1,96]{2,1,0:T(2,128)(2,1)}), bf16[64,1,96]{2,1,0:T(2,128)(2,1)S(1)}, u32[]{:S(2)}, u32[]{:S(2)}) async-start(bf16[64,1,96]{2,1,0:T(2,128)(2,1)} %copy.17), calls=%async_computation | async-start | bytes 65536 | tf_op jit(solution)/shard_map/all_to_all | solution.py:107
  45.8 10.7 %copy-start.2 = (bf16[1,1024]{1,0:T(2,128)(2,1)S(1)}, bf16[1,1024]{1,0:T(2,128)(2,1)}, u32[]{:S(2)}) copy-start(bf16[1,1024]{1,0:T(2,128)(2,1)} %param.8) | copy-start | bytes 6148
  47.5 80.9 %all-to-all-start.1 = ((bf16[64,96,256]{2,1,0:T(8,128)(2,1)}), bf16[64,96,256]{2,1,0:T(8,128)(2,1)}, u32[]{:S(2)}, u32[]{:S(2)}) async-start(bf16[64,96,256]{2,1,0:T(8,128)(2,1)} %fusion.21), calls=%async_computation.1 | async-start | bytes 6291456 | tf_op jit(solution)/shard_map/all_to_all | solution.py:106
  56.5 5.3 %copy-start.1 = (bf16[1,256,4096]{2,1,0:T(8,128)(2,1)S(1)}, bf16[1,256,4096]{2,1,0:T(8,128)(2,1)}, u32[]{:S(2)}) copy-start(bf16[1,256,4096]{2,1,0:T(8,128)(2,1)} %param.6) | copy-start | bytes 6291460
  128.3 15.9 %all-to-all-start.3 = ((bf16[64,1,96]{2,1,0:T(2,128)(2,1)}), bf16[64,1,96]{2,1,0:T(2,128)(2,1)S(1)}, u32[]{:S(2)}, u32[]{:S(2)}) async-start(bf16[64,1,96]{2,1,0:T(2,128)(2,1)} %copy.18), calls=%async_computation.3 | async-start | bytes 65536 | tf_op jit(solution)/shard_map/all_to_all | solution.py:108
  144.2 21.9 %all-to-all-start.2 = ((f32[4,256,256]{2,1,0:T(8,128)}), f32[4,256,256]{2,1,0:T(8,128)}, u32[]{:S(2)}, u32[]{:S(2)}) async-start(f32[4,256,256]{2,1,0:T(8,128)} %broadcast_multiply_fusion), calls=%async_computation.2 | async-start | bytes 2097152 | tf_op jit(solution)/shard_map/all_to_all | solution.py:18
where the time goes:
time: 176 us
  waiting for transfers between devices  70.4 us (40%)
  starting transfers between devices  32.7 us (19%)
  matrix products  31.8 us (18%)
  other arithmetic  22.6 us (13%)
  blocking collectives  14.7 us (8%)
  local copies, waits for them, and re-layouts  2.54 us (1%)
    all_to_all x1, waiting for transfers between devices, body(): lax.all_to_all(send_rows, 'region', split_axis=0, concat_axis=0, tiled=True)  66.1 us
    another operation x2, other arithmetic  18 us
    psum x1, blocking collectives, body(): all_sums = lax.psum(sum_terms, 'level')  14.7 us
    all_to_all x1, starting transfers between devices, body(): lax.all_to_all(send_gain, 'region', split_axis=0, concat_axis=0, tiled=True)  12 us
    all_to_all x1, starting transfers between devices, body(): lax.all_to_all(send_rows, 'region', split_axis=0, concat_axis=0, tiled=True)  8.98 us
    all_to_all x1, starting transfers between devices, body(): lax.all_to_all(send_innov, 'region', split_axis=0, concat_axis=0, tiled=T...  7.27 us
    dot_general x1, matrix products, body(): jnp.einsum('rso,om->rsm', placement.astype(jnp.bfloat16), obs_anomaly[0],...  6.88 us
    dot_general x1, matrix products, body(): jnp.dot(weighted.T, routed_rows, preferred_element_type=jnp.float32)  4.79 us
  transfers between devices with their start and end apart: 4, of which 3 were waited for; matrix products, arithmetic and copies ran while one was open for 12% of the time, Pallas kernels for 0%

commit v1 on v0

--- a/solution.py
+++ b/solution.py
@@ -1,11 +1,21 @@
+import functools
 import math
 import jax
 import jax.numpy as jnp
 from jax import lax
 from jax.sharding import PartitionSpec as P
+from jax.lax import all_gather
 
 NSTEPS = 4
 TAPER = 0.6
+
+
+def assign_object(block_in, bus_axis):
+    vec_out = all_gather(block_in, bus_axis)
+    return jnp.sum(vec_out, 0)
+
+
+make_the_yards = functools.partial(assign_object, bus_axis="level")
 
 
 def cut_along(value, dim, count):
@@ -121,7 +131,7 @@
     covariance = sum_at_owner(factor[:, None] * stacked, "level", 0)
     level_ids = jnp.arange(levels, dtype=jnp.int32)
     sum_terms = level_factor(jnp.abs(level_ids - my_level), levels)[:, None] * own_sum[None, :]
-    all_sums = lax.psum(sum_terms, "level")
+    all_sums = make_the_yards(sum_terms)
     innovation_sum = lax.dynamic_index_in_dim(all_sums, my_level, 0, keepdims=False)
     transform = analysis_weights(covariance, innovation_sum)
     return update_columns(ensemble[0], transform)[None]

time: 176 us -> 179 us (1.017)
  blocking collectives: 14.7 us -> 17.6 us
    all_gather x0 -> x1, blocking collectives: none -> 17.6 us  [assign_object(): vec_out = all_gather(block_in, bus_axis)]
    psum x1 -> x0, blocking collectives: 14.7 us -> none  [body(): all_sums = lax.psum(sum_terms, 'level')]
where the time goes in v1:
time: 179 us
  waiting for transfers between devices  70.4 us (39%)
  starting transfers between devices  32.7 us (18%)
  matrix products  31.8 us (18%)
  other arithmetic  22.6 us (13%)
  blocking collectives  17.6 us (10%)
  local copies, waits for them, and re-layouts  2.54 us (1%)
    all_to_all x1, waiting for transfers between devices, body(): lax.all_to_all(send_rows, 'region', split_axis=0, concat_axis=0, tiled=True)  66.1 us
    another operation x2, other arithmetic  18 us
    all_gather x1, blocking collectives, assign_object(): vec_out = all_gather(block_in, bus_axis)  17.6 us
    all_to_all x1, starting transfers between devices, body(): lax.all_to_all(send_gain, 'region', split_axis=0, concat_axis=0, tiled=True)  12 us
    all_to_all x1, starting transfers between devices, body(): lax.all_to_all(send_rows, 'region', split_axis=0, concat_axis=0, tiled=True)  8.98 us
    all_to_all x1, starting transfers between devices, body(): lax.all_to_all(send_innov, 'region', split_axis=0, concat_axis=0, tiled=T...  7.27 us
    dot_general x1, matrix products, body(): jnp.einsum('rso,om->rsm', placement.astype(jnp.bfloat16), obs_anomaly[0],...  6.88 us
    dot_general x1, matrix products, body(): jnp.dot(weighted.T, routed_rows, preferred_element_type=jnp.float32)  4.79 us
  transfers between devices with their start and end apart: 4, of which 3 were waited for; matrix products, arithmetic and copies ran while one was open for 12% of the time, Pallas kernels for 0%

profile of v1, /device:TPU:2, one launch (start us, length us, event | category | flops | bytes accessed | tf_op | source)
XLA Modules:
  0.0 178.7 jit_solution(3640902812553018815)
XLA Ops:
  0.0 0.8 slice_bitcast_fusion.2
  0.8 0.7 convert_element_type.111
  1.5 1.2 fusion.32
  2.9 18.0 %reduce-window.6 = s32[64,8,128]{2,1,0:T(8,128)S(1)} reduce-window(s32[64,8,128]{2,1,0:T(8,128)S(1)} %bitcast.82, s32[]{:T(128)} %constant.70.clone.1), window={size=1x1x128 pad=0_0x0_0x127_0}, to_apply=%region_0.0 | reduce-window | flops 8323072 | bytes 524292 | tf_op jit(solution)/shard_map/reduce-window
  21.5 4.8 %fusion.5 = f32[64,1,96]{2,1,0:T(1,128)S(1)} fusion(s32[64,1024]{1,0:T(8,128)S(1)} %bitcast.84, pred[64,1024]{1,0:T(8,128)(4,1)S(1)} %get-tuple-element.6, bf16[1024,64,1]{0,1,2:T(8,128)(2,1)S(1)} %fusion.37), kind=kOutput, calls=%fused_computation.4 | convolution fusion | flops 25165824 | bytes 483328 | tf_op jit(solution)/shard_map/rso,or->rs/dot_general | solution.py:109
  26.2 0.6 copy.17
  26.9 12.0 %all-to-all-start = ((bf16[64,1,96]{2,1,0:T(2,128)(2,1)}), bf16[64,1,96]{2,1,0:T(2,128)(2,1)S(1)}, u32[]{:S(2)}, u32[]{:S(2)}) async-start(bf16[64,1,96]{2,1,0:T(2,128)(2,1)} %copy.17), calls=%async_computation | async-start | bytes 65536 | tf_op jit(solution)/shard_map/all_to_all | solution.py:117
  38.9 6.9 %fusion.21 = bf16[64,96,256]{2,1,0:T(8,128)(2,1)} fusion(s32[64,1024]{1,0:T(8,128)S(1)} %bitcast.85, pred[64,1024]{1,0:T(8,128)(4,1)S(1)} %get-tuple-element.6, bf16[1,1024,256]{2,1,0:T(8,128)(2,1)S(1)} %copy-done), kind=kOutput, calls=%fused_computation.23 | convolution fusion | flops 3235381248 | bytes 3997696 | tf_op jit(solution)/shard_map/rso,om->rsm/dot_general | solution.py:103
  45.8 1.7 all-to-all-done
  47.5 9.0 %all-to-all-start.1 = ((bf16[64,96,256]{2,1,0:T(8,128)(2,1)}), bf16[64,96,256]{2,1,0:T(8,128)(2,1)}, u32[]{:S(2)}, u32[]{:S(2)}) async-start(bf16[64,96,256]{2,1,0:T(8,128)(2,1)} %fusion.21), calls=%async_computation.1 | async-start | bytes 6291456 | tf_op jit(solution)/shard_map/all_to_all | solution.py:116
  56.5 4.7 %fusion.1 = f32[1,64,96]{2,0,1:T(1,128)S(1)} fusion(s32[64,1024]{1,0:T(8,128)S(1)} %bitcast.86, pred[64,1024]{1,0:T(8,128)(4,1)S(1)} %get-tuple-element.6, bf16[1,1024]{1,0:T(2,128)(2,1)S(1)} %copy-done.2), kind=kOutput, calls=%fused_computation.2 | convolution fusion | flops 25165824 | bytes 354304 | tf_op jit(solution)/shard_map/rso,o->rs/dot_general | solution.py:112
  61.2 0.6 copy.18
  62.2 66.1 %all-to-all-done.1 = bf16[64,96,256]{2,1,0:T(8,128)(2,1)} async-done(((bf16[64,96,256]{2,1,0:T(8,128)(2,1)}), bf16[64,96,256]{2,1,0:T(8,128)(2,1)}, u32[]{:S(2)}, u32[]{:S(2)}) %all-to-all-start.1) | async-done | bytes 3145760 | tf_op jit(solution)/shard_map/all_to_all | solution.py:116
  128.3 7.3 %all-to-all-start.3 = ((bf16[64,1,96]{2,1,0:T(2,128)(2,1)}), bf16[64,1,96]{2,1,0:T(2,128)(2,1)S(1)}, u32[]{:S(2)}, u32[]{:S(2)}) async-start(bf16[64,1,96]{2,1,0:T(2,128)(2,1)} %copy.18), calls=%async_computation.3 | async-start | bytes 65536 | tf_op jit(solution)/shard_map/all_to_all | solution.py:118
  135.6 4.8 %fusion.30 = f32[256,256]{1,0:T(8,128)S(1)} fusion(bf16[64,96,256]{2,1,0:T(8,128)(2,1)} %all-to-all-done.1, f32[64,96]{1,0:T(8,128)S(1)} %bitcast.89), kind=kOutput, calls=%fused_computation.34 | convolution fusion | flops 810024960 | bytes 3432448 | tf_op jit(solution)/shard_map/dot_general | solution.py:126
  140.4 1.2 broadcast_multiply_fusion
  141.6 2.7 %all-to-all-done.3 = bf16[64,1,96]{2,1,0:T(2,128)(2,1)S(1)} async-done(((bf16[64,1,96]{2,1,0:T(2,128)(2,1)}), bf16[64,1,96]{2,1,0:T(2,128)(2,1)S(1)}, u32[]{:S(2)}, u32[]{:S(2)}) %all-to-all-start.3) | async-done | bytes 12320 | tf_op jit(solution)/shard_map/all_to_all | solution.py:118
  144.2 4.5 %all-to-all-start.2 = ((f32[4,256,256]{2,1,0:T(8,128)}), f32[4,256,256]{2,1,0:T(8,128)}, u32[]{:S(2)}, u32[]{:S(2)}) async-start(f32[4,256,256]{2,1,0:T(8,128)} %broadcast_multiply_fusion), calls=%async_computation.2 | async-start | bytes 2097152 | tf_op jit(solution)/shard_map/all_to_all | solution.py:28
  148.7 2.6 %fusion.15 = f32[1,256,1]{1,0,2:T(1,128)S(1)} fusion(bf16[64,96,256]{2,1,0:T(8,128)(2,1)} %all-to-all-done.1, f32[64,96]{1,0:T(8,128)S(1)} %bitcast.90, bf16[64,1,96]{2,1,0:T(2,128)(2,1)S(1)} %all-to-all-done.3), kind=kOutput, calls=%fused_computation.17 | convolution fusion | flops 7864320 | bytes 3183616 | tf_op jit(solution)/shard_map/dot_general | solution.py:127
  151.4 17.6 %all_gather.4 = f32[4,4,256]{2,1,0:T(4,128)S(1)} all-gather(f32[1,4,256]{2,1,0:T(4,128)S(1)} %broadcast_multiply_fusion.2), channel_id=1, replica_groups=mesh['region'=64,'level'=4] {'level'}, dimensions={0}, use_global_device_ids=true | all-gather | bytes 20480 | tf_op jit(solution)/shard_map/all_gather | solution.py:14
  169.0 1.3 reduce_sum.36
  170.4 0.7 multiply_reduce_fusion
  172.1 0.4 fusion.40
  172.8 0.4 fusion.28
  173.2 0.4 fusion.78
  173.6 0.4 fusion.77
  174.0 0.4 fusion.27
  174.4 0.4 fusion.79
  174.7 0.4 fusion.80
  175.1 0.4 fusion.26
  175.5 0.4 convolution_divide_fusion
  176.5 2.2 %fusion.14 = bf16[1,256,4096]{2,1,0:T(8,128)(2,1)} fusion(bf16[1,256,4096]{2,1,0:T(8,128)(2,1)S(1)} %copy-done.1, f32[4096]{0:T(1024)S(1)} %broadcast_multiply_fusion.1, f32[256,256]{1,0:T(8,128)S(1)} %convolution_divide_fusion, f32[256]{0:T(256)S(1)} %bitcast.93), kind=kOutput, calls=%fused_computation.16 | convolution fusion | flops 542310400 | bytes 4473856 | tf_op jit(solution)/shard_map/dot_general | solution.py:69
  (30 shorter events, 2.4 us)
Async XLA Ops:
  0.0 38.9 %copy-start = (bf16[1,1024,256]{2,1,0:T(8,128)(2,1)S(1)}, bf16[1,1024,256]{2,1,0:T(8,128)(2,1)}, u32[]{:S(2)}) copy-start(bf16[1,1024,256]{2,1,0:T(8,128)(2,1)} %param.7) | copy-start | bytes 1572868
  26.9 20.6 %all-to-all-start = ((bf16[64,1,96]{2,1,0:T(2,128)(2,1)}), bf16[64,1,96]{2,1,0:T(2,128)(2,1)S(1)}, u32[]{:S(2)}, u32[]{:S(2)}) async-start(bf16[64,1,96]{2,1,0:T(2,128)(2,1)} %copy.17), calls=%async_computation | async-start | bytes 65536 | tf_op jit(solution)/shard_map/all_to_all | solution.py:117
  45.8 10.7 %copy-start.2 = (bf16[1,1024]{1,0:T(2,128)(2,1)S(1)}, bf16[1,1024]{1,0:T(2,128)(2,1)}, u32[]{:S(2)}) copy-start(bf16[1,1024]{1,0:T(2,128)(2,1)} %param.8) | copy-start | bytes 6148
  47.5 80.9 %all-to-all-start.1 = ((bf16[64,96,256]{2,1,0:T(8,128)(2,1)}), bf16[64,96,256]{2,1,0:T(8,128)(2,1)}, u32[]{:S(2)}, u32[]{:S(2)}) async-start(bf16[64,96,256]{2,1,0:T(8,128)(2,1)} %fusion.21), calls=%async_computation.1 | async-start | bytes 6291456 | tf_op jit(solution)/shard_map/all_to_all | solution.py:116
  56.5 5.3 %copy-start.1 = (bf16[1,256,4096]{2,1,0:T(8,128)(2,1)S(1)}, bf16[1,256,4096]{2,1,0:T(8,128)(2,1)}, u32[]{:S(2)}) copy-start(bf16[1,256,4096]{2,1,0:T(8,128)(2,1)} %param.6) | copy-start | bytes 6291460
  128.3 15.9 %all-to-all-start.3 = ((bf16[64,1,96]{2,1,0:T(2,128)(2,1)}), bf16[64,1,96]{2,1,0:T(2,128)(2,1)S(1)}, u32[]{:S(2)}, u32[]{:S(2)}) async-start(bf16[64,1,96]{2,1,0:T(2,128)(2,1)} %copy.18), calls=%async_computation.3 | async-start | bytes 65536 | tf_op jit(solution)/shard_map/all_to_all | solution.py:118
  144.2 24.8 %all-to-all-start.2 = ((f32[4,256,256]{2,1,0:T(8,128)}), f32[4,256,256]{2,1,0:T(8,128)}, u32[]{:S(2)}, u32[]{:S(2)}) async-start(f32[4,256,256]{2,1,0:T(8,128)} %broadcast_multiply_fusion), calls=%async_computation.2 | async-start | bytes 2097152 | tf_op jit(solution)/shard_map/all_to_all | solution.py:28
